TPU v7x, 256 devices: a whole 4x4x8 slice. The times are simulated.
256 devices in a mesh: section: 4 (over y), ctx: 16 (over z, x_hi), tp: 4 (over x_lo, core).
Axes of the slice: x: 4 (x_hi: 2, x_lo: 2; x = x_hi * 2 + x_lo), y: 4, z: 8, core: 2. Of those that a mesh axis runs over, the one named last changes fastest.
Arguments:
- hidden_in: bfloat16 [4, 2048, 4096], P('section', 'ctx', 'tp'), may hold values from -16 to 16
- fresh_in: bfloat16 [3, 2048, 4096], P(None, 'ctx', 'tp'), may hold values from -16 to 16
- block_table: int32 [32], replicated, may hold values from 0 to 31, as said below
- norm_gain: float32 [4, 4096], P('section'), may hold values from 0.1 to 1.9
- w_query: bfloat16 [4, 4096, 4096], P('section', 'ctx', 'tp'), may hold values from -3.125 to 3.125
- w_key: bfloat16 [4, 4096, 512], P('section', 'ctx', 'tp'), may hold values from -0.09375 to 0.09375
- w_value: bfloat16 [4, 4096, 512], P('section', 'ctx', 'tp'), may hold values from -0.09375 to 0.09375
- w_out: bfloat16 [4, 4096, 4096], P('section', 'ctx', 'tp'), may hold values from -0.09375 to 0.09375
Outputs:
- layer_outputs: bfloat16 [4, 4, 2048, 4096], P(None, 'section', 'ctx', 'tp')
Inputs may be any that keep to these rules, and one draw needn't show every extreme that they name: `block_table`: slots 2i and 2i + 1 hold blocks p and 31 - p for some p, in either order; every block appears once.
All inputs are finite; a program needn't handle non-finite values.
Results may differ from a plain program's by a relative error of at most 0.03.
Values may be sent and summed in bfloat16 or wider, within the bound.
No kernel may reach another device: no remote copies, remote signals or barrier semaphores. Data moves between devices by JAX's collectives and lax.ppermute only.
A program may use at most 128 MiB of HBM per device.

v0:
```python
import jax
import jax.numpy as jnp
from jax import lax
from jax.sharding import PartitionSpec as P

HEAD_DIM = 128
BLOCK = 64
EPS = 1e-05
ROPE_BASE = 500000.0
NEGATIVE = -1e30


def shifted(x, axis, by):
    count = lax.axis_size(axis)
    pairs = [(i, i + by) for i in range(count) if 0 <= i + by < count]
    return lax.ppermute(x, axis, pairs)


def rotate(vectors, cosine_table, sine_table):
    half_width = vectors.shape[-1] // 2
    first_half = vectors[..., :half_width]
    second_half = vectors[..., half_width:]
    return jnp.concatenate(
        [
            first_half * cosine_table - second_half * sine_table,
            second_half * cosine_table + first_half * sine_table,
        ],
        axis=-1,
    )


def angle_tables(positions):
    half_width = HEAD_DIM // 2
    frequency = ROPE_BASE ** (-(jnp.arange(half_width, dtype=jnp.float32) * 2.0) / HEAD_DIM)
    angles = positions.astype(jnp.float32)[:, None] * frequency[None, :]
    return (jnp.cos(angles), jnp.sin(angles))


def block_positions(block_table, first_row, row_count):
    row_ids = first_row + jnp.arange(row_count, dtype=jnp.int32)
    slot_ids = row_ids // BLOCK
    matches = slot_ids[:, None] == jnp.arange(block_table.shape[0], dtype=jnp.int32)[None, :]
    owners = jnp.sum(jnp.where(matches, block_table[None, :], 0), axis=1)
    return owners * BLOCK + row_ids % BLOCK


def on_device(hidden_in, fresh_in, block_table, norm_gain, w_query, w_key, w_value, w_out):
    row_count = hidden_in.shape[1]
    sections = lax.axis_size("section")
    query_weights, key_weights, value_weights, output_weights = (
        lax.all_gather(w_query[0], "ctx", axis=0, tiled=True),
        lax.all_gather(w_key[0], "ctx", axis=0, tiled=True),
        lax.all_gather(w_value[0], "ctx", axis=0, tiled=True),
        lax.all_gather(w_out[0], "ctx", axis=0, tiled=True),
    )
    gain_row = norm_gain[0]
    positions = block_positions(block_table, lax.axis_index("ctx") * row_count, row_count)
    cosine_table, sine_table = angle_tables(positions)
    cosine_table = cosine_table[:, None, :]
    sine_table = sine_table[:, None, :]
    query_heads = query_weights.shape[1] // HEAD_DIM
    kv_local = key_weights.shape[1] // HEAD_DIM
    group_size = query_heads // kv_local
    score_scale = HEAD_DIM ** (-0.5)
    first_section = lax.axis_index("section") == 0
    produced = []
    current = hidden_in[0]
    for step_index in range(sections):
        full_rows = lax.all_gather(current, "tp", axis=1, tiled=True)
        widened = full_rows.astype(jnp.float32)
        normed = (
            widened
            * lax.rsqrt(jnp.mean(widened * widened, axis=-1, keepdims=True) + EPS)
            * gain_row
        ).astype(jnp.bfloat16)
        queries = jnp.dot(normed, query_weights, preferred_element_type=jnp.float32).reshape(
            row_count, query_heads, HEAD_DIM
        )
        queries = (
            rotate(queries, cosine_table, sine_table)
            .astype(jnp.bfloat16)
            .reshape(row_count, kv_local, group_size, HEAD_DIM)
        )
        key_vecs = jnp.dot(normed, key_weights, preferred_element_type=jnp.float32).reshape(
            row_count, kv_local, HEAD_DIM
        )
        key_vecs = (
            rotate(key_vecs, cosine_table, sine_table)
            .astype(jnp.bfloat16)
            .reshape(row_count, kv_local * HEAD_DIM)
        )
        values = jnp.dot(normed, value_weights, preferred_element_type=jnp.float32).astype(
            jnp.bfloat16
        )
        key_piece = lax.all_gather(key_vecs, "ctx", axis=0, tiled=True)
        value_piece = lax.all_gather(values, "ctx", axis=0, tiled=True)
        key_count = key_piece.shape[0]
        key_positions = block_positions(block_table, jnp.int32(0), key_count)
        scores = (
            jnp.einsum(
                "rkgd,nkd->kgrn",
                queries,
                key_piece.reshape(key_count, kv_local, HEAD_DIM),
                preferred_element_type=jnp.float32,
            )
            * score_scale
        )
        allowed = key_positions[None, None, None, :] <= positions[None, None, :, None]
        largest = jnp.full((kv_local, group_size, row_count), NEGATIVE, jnp.float32)
        new_largest = jnp.maximum(largest, jnp.max(jnp.where(allowed, scores, NEGATIVE), axis=-1))
        weights = jnp.where(allowed, jnp.exp(scores - new_largest[..., None]), 0.0)
        weight_sum = jnp.sum(weights, axis=-1)
        mixed = jnp.einsum(
            "kgrn,nkd->kgrd",
            weights.astype(jnp.bfloat16),
            value_piece.reshape(key_count, kv_local, HEAD_DIM),
            preferred_element_type=jnp.float32,
        )
        largest, weight_sum, accumulated = (new_largest, weight_sum, mixed)
        attended = (accumulated / weight_sum[..., None]).astype(jnp.bfloat16)
        attended = attended.transpose(2, 0, 1, 3).reshape(row_count, query_heads * HEAD_DIM)
        summed = lax.psum_scatter(
            lax.dot_general(
                attended,
                output_weights,
                (((1,), (1,)), ((), ())),
                preferred_element_type=jnp.float32,
            ).astype(jnp.bfloat16),
            "tp",
            scatter_dimension=1,
            tiled=True,
        ).astype(jnp.float32)
        result = (current.astype(jnp.float32) + summed).astype(jnp.bfloat16)
        produced.append(result)
        if step_index + 1 < sections:
            moved = shifted(result, "section", 1)
            current = jnp.where(first_section, fresh_in[step_index], moved)
    return jnp.stack(produced)[:, None]


def solution(mesh):
    in_specs = (
        P("section", "ctx", "tp"),
        P(None, "ctx", "tp"),
        P(),
        P("section", None),
        P("section", "ctx", "tp"),
        P("section", "ctx", "tp"),
        P("section", "ctx", "tp"),
        P("section", "ctx", "tp"),
    )
    out_specs = P(None, "section", "ctx", "tp")
    return jax.shard_map(
        on_device, mesh=mesh, in_specs=in_specs, out_specs=out_specs, check_vma=False
    )
```

profile of v0, /device:TPU:1, one launch (start us, length us, event | category | flops | bytes accessed | tf_op | source)
XLA Modules:
  0.0 1003.0 jit_solution(7136594776463280632)
XLA Ops:
  12.2 24.3 %all-gather.20.cloned.1.call-done = bf16[1,128,4096]{2,1,0:T(8,128)(2,1)} async-done(((bf16[1,128,1024]{2,1,0:T(8,128)(2,1)}), bf16[1,128,4096]{2,1,0:T(8,128)(2,1)}) %all-gather.20.cloned.1.call-update) | async-done | bytes 1048592 | tf_op jit(solution)/shard_map/all_gather | solution.py:69
  38.1 75.9 %all-gather.22.cloned.1.call-done = bf16[1,4096,128]{2,1,0:T(8,128)(2,1)} async-done(((bf16[1,256,128]{2,1,0:T(8,128)(2,1)}), bf16[1,4096,128]{2,1,0:T(8,128)(2,1)}) %all-gather.22.cloned.1.call-update) | async-done | bytes 1048592 | tf_op jit(solution)/shard_map/all_gather | solution.py:52
  114.0 2.2 convolution_bitcast_fusion.3
  116.4 33.2 %all_gather.50 = bf16[2048,128]{0,1:T(8,128)(2,1)S(1)} all-gather(bf16[128,128]{0,1:T(8,128)(2,1)S(1)} %pad_maximum_fusion), channel_id=1, replica_groups=mesh['section'=4,'ctx'=16,'tp'=4] {'ctx'}, dimensions={0}, use_global_device_ids=true | all-gather | bytes 557056 | tf_op jit(solution)/shard_map/all_gather | solution.py:95
  149.5 42.2 %all-gather.26.cloned.1.call-done = bf16[1,4096,128]{2,1,0:T(8,128)(2,1)} async-done(((bf16[1,256,128]{2,1,0:T(8,128)(2,1)}), bf16[1,4096,128]{2,1,0:T(8,128)(2,1)}) %all-gather.26.cloned.1.call-update) | async-done | bytes 1048592 | tf_op jit(solution)/shard_map/all_gather | solution.py:53
  191.8 2.1 convolution_convert_fusion.3
  193.8 34.4 %all_gather.53 = bf16[2048,128]{1,0:T(8,128)(2,1)S(1)} all-gather(bf16[128,128]{1,0:T(8,128)(2,1)S(1)} %convolution_convert_fusion.3), channel_id=1, replica_groups=mesh['section'=4,'ctx'=16,'tp'=4] {'ctx'}, dimensions={0}, use_global_device_ids=true | all-gather | bytes 557056 | tf_op jit(solution)/shard_map/all_gather | solution.py:96
  228.2 104.3 %all-gather.24.cloned.1.call-done = bf16[1,4096,1024]{2,1,0:T(8,128)(2,1)} async-done(((bf16[1,256,1024]{2,1,0:T(8,128)(2,1)}), bf16[1,4096,1024]{2,1,0:T(8,128)(2,1)}) %all-gather.24.cloned.1.call-update) | async-done | bytes 8388624 | tf_op jit(solution)/shard_map/all_gather | solution.py:51
  332.5 5.0 fusion.76
  339.6 1.7 fusion.28
  341.3 1.7 fusion.108
  343.0 123.9 %all-gather.28.cloned.1.call-done = bf16[1,4096,1024]{2,1,0:T(8,128)(2,1)} async-done(((bf16[1,256,1024]{2,1,0:T(8,128)(2,1)}), bf16[1,4096,1024]{2,1,0:T(8,128)(2,1)}) %all-gather.28.cloned.1.call-update) | async-done | bytes 8388624 | tf_op jit(solution)/shard_map/all_gather | solution.py:54
  466.9 7.2 fusion.36
  474.3 21.0 %reduce-scatter.5.cloned.1.call-done = bf16[128,1024]{1,0:T(8,128)(2,1)} async-done(((bf16[128,4096]{1,0:T(8,128)(2,1)}), bf16[128,1024]{1,0:T(8,128)(2,1)}) %reduce-scatter.5.cloned.1.call-update) | async-done | bytes 262160 | tf_op jit(solution)/shard_map/reduce_scatter | solution.py:122
  496.3 3.1 collective-permute-start
  499.4 5.5 collective-permute-done
  506.9 25.8 %all-gather.14.cloned.1.call-done = bf16[128,4096]{1,0:T(8,128)(2,1)} async-done(((bf16[128,1024]{1,0:T(8,128)(2,1)}), bf16[128,4096]{1,0:T(8,128)(2,1)}) %all-gather.14.cloned.1.call-update) | async-done | bytes 1048592 | tf_op jit(solution)/shard_map/all_gather | solution.py:69
  534.3 2.2 convolution_bitcast_fusion.2
  536.7 7.1 fusion.24
  544.1 37.0 %all_gather.56 = bf16[2048,128]{0,1:T(8,128)(2,1)S(1)} all-gather(bf16[128,128]{0,1:T(8,128)(2,1)S(1)} %pad_maximum_fusion.1), channel_id=1, replica_groups=mesh['section'=4,'ctx'=16,'tp'=4] {'ctx'}, dimensions={0}, use_global_device_ids=true | all-gather | bytes 557056 | tf_op jit(solution)/shard_map/all_gather | solution.py:95
  581.1 1.7 convolution_convert_fusion.2
  582.8 32.2 %all_gather.57 = bf16[2048,128]{1,0:T(8,128)(2,1)S(1)} all-gather(bf16[128,128]{1,0:T(8,128)(2,1)S(1)} %convolution_convert_fusion.2), channel_id=1, replica_groups=mesh['section'=4,'ctx'=16,'tp'=4] {'ctx'}, dimensions={0}, use_global_device_ids=true | all-gather | bytes 557056 | tf_op jit(solution)/shard_map/all_gather | solution.py:96
  617.0 1.7 fusion.30
  618.7 1.7 fusion.102
  621.0 3.9 fusion.39
  625.0 34.8 %reduce-scatter.7.cloned.1.call-done = bf16[128,1024]{1,0:T(8,128)(2,1)} async-done(((bf16[128,4096]{1,0:T(8,128)(2,1)}), bf16[128,1024]{1,0:T(8,128)(2,1)}) %reduce-scatter.7.cloned.1.call-update) | async-done | bytes 262160 | tf_op jit(solution)/shard_map/reduce_scatter | solution.py:122
  660.8 3.1 collective-permute-start.1
  663.9 5.5 collective-permute-done.1
  671.2 26.0 %all-gather.16.cloned.1.call-done = bf16[128,4096]{1,0:T(8,128)(2,1)} async-done(((bf16[128,1024]{1,0:T(8,128)(2,1)}), bf16[128,4096]{1,0:T(8,128)(2,1)}) %all-gather.16.cloned.1.call-update) | async-done | bytes 1048592 | tf_op jit(solution)/shard_map/all_gather | solution.py:69
  698.8 1.8 convolution_bitcast_fusion.1
  700.9 7.1 fusion.22
  708.3 37.4 %all_gather.59 = bf16[2048,128]{0,1:T(8,128)(2,1)S(1)} all-gather(bf16[128,128]{0,1:T(8,128)(2,1)S(1)} %pad_maximum_fusion.2), channel_id=1, replica_groups=mesh['section'=4,'ctx'=16,'tp'=4] {'ctx'}, dimensions={0}, use_global_device_ids=true | all-gather | bytes 557056 | tf_op jit(solution)/shard_map/all_gather | solution.py:95
  745.7 1.7 convolution_convert_fusion.1
  747.5 34.1 %all_gather.60 = bf16[2048,128]{1,0:T(8,128)(2,1)} all-gather(bf16[128,128]{1,0:T(8,128)(2,1)S(1)} %convolution_convert_fusion.1), channel_id=1, replica_groups=mesh['section'=4,'ctx'=16,'tp'=4] {'ctx'}, dimensions={0}, use_global_device_ids=true | all-gather | bytes 557056 | tf_op jit(solution)/shard_map/all_gather | solution.py:96
  783.5 1.7 fusion.32
  787.5 3.9 fusion.42
  791.5 35.3 %reduce-scatter.9.cloned.1.call-done = bf16[128,1024]{1,0:T(8,128)(2,1)} async-done(((bf16[128,4096]{1,0:T(8,128)(2,1)}), bf16[128,1024]{1,0:T(8,128)(2,1)}) %reduce-scatter.9.cloned.1.call-update) | async-done | bytes 262160 | tf_op jit(solution)/shard_map/reduce_scatter | solution.py:122
  827.8 3.1 collective-permute-start.2
  830.9 5.5 collective-permute-done.2
  838.2 26.0 %all-gather.18.cloned.1.call-done = bf16[128,4096]{1,0:T(8,128)(2,1)} async-done(((bf16[128,1024]{1,0:T(8,128)(2,1)}), bf16[128,4096]{1,0:T(8,128)(2,1)}) %all-gather.18.cloned.1.call-update) | async-done | bytes 1048592 | tf_op jit(solution)/shard_map/all_gather | solution.py:69
  865.8 2.2 convolution_bitcast_fusion
  868.2 7.1 fusion.20
  875.6 37.0 %all_gather.62 = bf16[2048,128]{0,1:T(8,128)(2,1)S(1)} all-gather(bf16[128,128]{0,1:T(8,128)(2,1)S(1)} %pad_maximum_fusion.3), channel_id=1, replica_groups=mesh['section'=4,'ctx'=16,'tp'=4] {'ctx'}, dimensions={0}, use_global_device_ids=true | all-gather | bytes 557056 | tf_op jit(solution)/shard_map/all_gather | solution.py:95
  912.6 1.7 convolution_convert_fusion
  914.4 34.2 %all_gather.63 = bf16[2048,128]{1,0:T(8,128)(2,1)} all-gather(bf16[128,128]{1,0:T(8,128)(2,1)S(1)} %convolution_convert_fusion), channel_id=1, replica_groups=mesh['section'=4,'ctx'=16,'tp'=4] {'ctx'}, dimensions={0}, use_global_device_ids=true | all-gather | bytes 557056 | tf_op jit(solution)/shard_map/all_gather | solution.py:96
  950.5 1.7 fusion.34
  954.6 3.9 fusion.45
  958.5 35.3 %reduce-scatter.11.cloned.1.call-done = bf16[128,1024]{1,0:T(8,128)(2,1)} async-done(((bf16[128,4096]{1,0:T(8,128)(2,1)}), bf16[128,1024]{1,0:T(8,128)(2,1)}) %reduce-scatter.11.cloned.1.call-update) | async-done | bytes 262160 | tf_op jit(solution)/shard_map/reduce_scatter | solution.py:122
  (133 shorter events, 37.0 us)
Async XLA Ops:
  6.5 326.0 %copy-start.9 = (f32[1,4096]{1,0:T(1,128)S(1)}, f32[1,4096]{1,0:T(1,128)}, u32[]{:S(2)}) copy-start(f32[1,4096]{1,0:T(1,128)} %param.11) | copy-start | bytes 49156
  6.5 30.0 %all-gather.20.cloned.1.call-start = ((), (), s32[]{:S(2)}) async-start(), calls=%async_computation.11 | async-start | bytes 1310720 | tf_op jit(solution)/shard_map/all_gather | solution.py:69
  7.3 106.7 %all-gather.22.cloned.1.call-start = ((), (), s32[]{:S(2)}) async-start(), calls=%async_computation.12 | async-start | bytes 1114112 | tf_op jit(solution)/shard_map/all_gather | solution.py:52
  8.0 183.8 %all-gather.26.cloned.1.call-start = ((), (), s32[]{:S(2)}) async-start(), calls=%async_computation.14 | async-start | bytes 1114112 | tf_op jit(solution)/shard_map/all_gather | solution.py:53
  8.7 323.8 %all-gather.24.cloned.1.call-start = ((), (), s32[]{:S(2)}) async-start(), calls=%async_computation.13 | async-start | bytes 8912896 | tf_op jit(solution)/shard_map/all_gather | solution.py:51
  9.3 457.6 %all-gather.28.cloned.1.call-start = ((), (), s32[]{:S(2)}) async-start(), calls=%async_computation.15 | async-start | bytes 8912896 | tf_op jit(solution)/shard_map/all_gather | solution.py:54
  9.9 485.3 %reduce-scatter.5.cloned.1.call-start = ((), (), s32[]{:S(2)}) async-start(), calls=%async_computation.4 | async-start | bytes 1310720 | tf_op jit(solution)/shard_map/reduce_scatter | solution.py:122
  10.0 526.5 %copy-start.13 = (f32[64]{0:T(128)}, f32[64]{0:T(128)S(1)}, u32[]{:S(2)}) copy-start(f32[64]{0:T(128)S(1)} %multiply_power_fusion) | copy-start | bytes 772
  11.5 524.9 %copy-start.10 = (f32[128]{0:T(128)}, f32[128]{0:T(128)S(1)}, u32[]{:S(2)}) copy-start(f32[128]{0:T(128)S(1)} %get-tuple-element.5) | copy-start | bytes 1540
  343.0 152.2 %copy-start.6 = (bf16[1,128,1024]{2,1,0:T(8,128)(2,1)S(1)}, bf16[1,128,1024]{2,1,0:T(8,128)(2,1)}, u32[]{:S(2)}) copy-start(bf16[1,128,1024]{2,1,0:T(8,128)(2,1)} %param.8) | copy-start | bytes 786436
  474.2 58.4 %all-gather.14.cloned.1.call-start = ((), (), s32[]{:S(2)}) async-start(), calls=%async_computation.5 | async-start | bytes 1310720 | tf_op jit(solution)/shard_map/all_gather | solution.py:69
  496.3 8.7 collective-permute-start
  506.7 153.1 %reduce-scatter.7.cloned.1.call-start = ((), (), s32[]{:S(2)}) async-start(), calls=%async_computation.6 | async-start | bytes 1310720 | tf_op jit(solution)/shard_map/reduce_scatter | solution.py:122
  532.7 48.4 %copy-start.1 = (bf16[128,4096]{1,0:T(8,128)(2,1)S(1)}, bf16[128,4096]{1,0:T(8,128)(2,1)}, u32[]{:S(2)}) copy-start(bf16[128,4096]{1,0:T(8,128)(2,1)} %all-gather.14.cloned.1.call-done) | copy-start | bytes 3145732
  617.0 3.5 slice-start
  618.7 2.3 slice-start.1
  620.4 39.4 %copy-start.4 = (bf16[128,1024]{1,0:T(8,128)(2,1)S(1)}, bf16[128,1024]{1,0:T(8,128)(2,1)}, u32[]{:S(2)}) copy-start(bf16[128,1024]{1,0:T(8,128)(2,1)} %bitcast_select_fusion.6) | copy-start | bytes 786436
  620.4 78.4 %copy-start.17 = (bf16[1,4096,128]{2,1,0:T(8,128)(2,1)S(1)}, bf16[1,4096,128]{2,1,0:T(8,128)(2,1)}, u32[]{:S(2)}) copy-start(bf16[1,4096,128]{2,1,0:T(8,128)(2,1)} %all-gather.22.cloned.1.call-done) | copy-start | bytes 3145732
  620.5 80.2 %copy-start.11 = (f32[128]{0:T(128)S(1)}, f32[128]{0:T(128)}, u32[]{:S(2)}) copy-start(f32[128]{0:T(128)} %copy-done.10) | copy-start | bytes 1540
  620.5 80.2 %copy-start.14 = (f32[64]{0:T(128)S(1)}, f32[64]{0:T(128)}, u32[]{:S(2)}) copy-start(f32[64]{0:T(128)} %copy-done.13) | copy-start | bytes 772
  624.9 72.3 %all-gather.16.cloned.1.call-start = ((), (), s32[]{:S(2)}) async-start(), calls=%async_computation.7 | async-start | bytes 1310720 | tf_op jit(solution)/shard_map/all_gather | solution.py:69
  660.8 8.6 collective-permute-start.1
  671.2 155.6 %reduce-scatter.9.cloned.1.call-start = ((), (), s32[]{:S(2)}) async-start(), calls=%async_computation.8 | async-start | bytes 1310720 | tf_op jit(solution)/shard_map/reduce_scatter | solution.py:122
  697.2 48.5 %copy-start.2 = (bf16[128,4096]{1,0:T(8,128)(2,1)S(1)}, bf16[128,4096]{1,0:T(8,128)(2,1)}, u32[]{:S(2)}) copy-start(bf16[128,4096]{1,0:T(8,128)(2,1)} %all-gather.16.cloned.1.call-done) | copy-start | bytes 3145732
  781.9 3.3 copy-start.8
  783.5 3.5 slice-start.2
  785.2 2.3 slice-start.3
  786.9 39.8 %copy-start.5 = (bf16[128,1024]{1,0:T(8,128)(2,1)S(1)}, bf16[128,1024]{1,0:T(8,128)(2,1)}, u32[]{:S(2)}) copy-start(bf16[128,1024]{1,0:T(8,128)(2,1)} %bitcast_select_fusion.5) | copy-start | bytes 786436
  786.9 81.0 %copy-start.12 = (f32[128]{0:T(128)S(1)}, f32[128]{0:T(128)}, u32[]{:S(2)}) copy-start(f32[128]{0:T(128)} %copy-done.10) | copy-start | bytes 1540
  786.9 81.0 %copy-start.15 = (f32[64]{0:T(128)S(1)}, f32[64]{0:T(128)}, u32[]{:S(2)}) copy-start(f32[64]{0:T(128)} %copy-done.13) | copy-start | bytes 772
  791.4 72.8 %all-gather.18.cloned.1.call-start = ((), (), s32[]{:S(2)}) async-start(), calls=%async_computation.9 | async-start | bytes 1310720 | tf_op jit(solution)/shard_map/all_gather | solution.py:69
  827.8 8.7 collective-permute-start.2
  838.1 155.6 %reduce-scatter.11.cloned.1.call-start = ((), (), s32[]{:S(2)}) async-start(), calls=%async_computation.10 | async-start | bytes 1310720 | tf_op jit(solution)/shard_map/reduce_scatter | solution.py:122
  864.2 48.4 %copy-start = (bf16[128,4096]{1,0:T(8,128)(2,1)S(1)}, bf16[128,4096]{1,0:T(8,128)(2,1)}, u32[]{:S(2)}) copy-start(bf16[128,4096]{1,0:T(8,128)(2,1)} %all-gather.18.cloned.1.call-done) | copy-start | bytes 3145732
  865.8 9.5 copy-start.16
  949.0 3.3 copy-start.7
  950.5 3.5 slice-start.4
  952.3 2.3 slice-start.5
  954.0 39.8 %copy-start.3 = (bf16[128,1024]{1,0:T(8,128)(2,1)S(1)}, bf16[128,1024]{1,0:T(8,128)(2,1)}, u32[]{:S(2)}) copy-start(bf16[128,1024]{1,0:T(8,128)(2,1)} %bitcast_select_fusion.4) | copy-start | bytes 786436
Sparse Core Ops, SparseCore 0:
  9.1 27.3 all-gather.19
  39.1 74.7 all-gather.21
  116.6 75.1 all-gather.25
  194.2 138.2 all-gather.23
  334.9 131.9 all-gather.27
  474.3 20.8 reduce-scatter.4
  506.8 25.8 all-gather.13
  625.1 34.6 reduce-scatter.6
  671.3 25.8 all-gather.15
  791.5 35.1 reduce-scatter.8
  838.3 25.8 all-gather.17
  958.6 35.1 reduce-scatter.10
where the time goes:
time: 1010 us; the launch traced here: 1000 us
  waiting for transfers between devices  595 us (59%)
  blocking collectives  280 us (28%)
  matrix products  73.8 us (7%)
  other arithmetic  27.1 us (3%)
  between operations  14.5 us (1%)
    all_gather x4, blocking collectives, on_device(): key_piece = lax.all_gather(key_vecs, 'ctx', axis=0, tiled=True)  145 us
    all_gather x4, blocking collectives, on_device(): value_piece = lax.all_gather(values, 'ctx', axis=0, tiled=True)  135 us
    reduce_scatter x4, waiting for transfers between devices, on_device(): lax.psum_scatter(lax.dot_general(attended, output_weights, (((1,), (1,)),...  126 us
    all_gather x1, waiting for transfers between devices, on_device(): lax.all_gather(w_out[0], 'ctx', axis=0, tiled=True)  124 us
    all_gather x1, waiting for transfers between devices, on_device(): lax.all_gather(w_query[0], 'ctx', axis=0, tiled=True)  104 us
    all_gather x4, waiting for transfers between devices, on_device(): full_rows = lax.all_gather(current, 'tp', axis=1, tiled=True)  102 us
    all_gather x1, waiting for transfers between devices, on_device(): lax.all_gather(w_key[0], 'ctx', axis=0, tiled=True)  75.9 us
    all_gather x1, waiting for transfers between devices, on_device(): lax.all_gather(w_value[0], 'ctx', axis=0, tiled=True)  42.2 us
  transfers between devices with their start and end apart: 15, of which 15 were waited for; matrix products, arithmetic and copies ran while one was open for 2% of the time, Pallas kernels for 0%

commit v1 on v0

--- a/solution.py
+++ b/solution.py
@@ -48,7 +48,9 @@
     row_count = hidden_in.shape[1]
     sections = lax.axis_size("section")
     query_weights, key_weights, value_weights, output_weights = (
-        lax.all_gather(w_query[0], "ctx", axis=0, tiled=True),
+        jnp.concatenate(
+            lax.all_to_all(jnp.stack([w_query[0]] * lax.axis_size("ctx")), "ctx", 0, 0), axis=0
+        ),
         lax.all_gather(w_key[0], "ctx", axis=0, tiled=True),
         lax.all_gather(w_value[0], "ctx", axis=0, tiled=True),
         lax.all_gather(w_out[0], "ctx", axis=0, tiled=True),

time: 1010 us -> 942 us (0.933)
  waiting for transfers between devices: 595 us -> 476 us
  local copies, waits for them, and re-layouts: 3.35 us -> 31.2 us
  blocking collectives: 280 us -> 307 us
  starting transfers between devices: 9.98 us -> 22.4 us
  matrix products: 73.8 us -> 63.5 us
    all_gather x1 -> x0, waiting for transfers between devices: 104 us -> none  [on_device(): lax.all_gather(w_query[0], 'ctx', axis=0, tiled=True)]
    all_gather x1, waiting for transfers between devices: 75.9 us -> 135 us  [on_device(): lax.all_gather(w_key[0], 'ctx', axis=0, tiled=True)]
    all_gather x1, waiting for transfers between devices: 124 us -> 68.7 us  [on_device(): lax.all_gather(w_out[0], 'ctx', axis=0, tiled=True)]
    all_gather x4, blocking collectives: 145 us -> 176 us  [on_device(): key_piece = lax.all_gather(key_vecs, 'ctx', axis=0, tiled=True)]
    all_to_all x0 -> x1, local copies, waits for them, and re-layouts: none -> 12.3 us  [on_device(): lax.all_to_all(jnp.stack([w_query[0]] * lax.axis_size('ctx')), 'ctx', 0, 0)]
    all_to_all x0 -> x1, starting transfers between devices: none -> 11.8 us  [on_device(): lax.all_to_all(jnp.stack([w_query[0]] * lax.axis_size('ctx')), 'ctx', 0, 0)]
    dot_general x0 -> x1, local copies, waits for them, and re-layouts: none -> 11.7 us  [on_device(): jnp.dot(normed, query_weights, preferred_element_type=jnp.float32)]
  transfers between devices with their start and end apart: 15 -> 15, of which waited for: 15 -> 14; matrix products, arithmetic and copies ran while one was open for 2% -> 5% of each run, Pallas kernels for 0% -> 0%
where the time goes in v1:
time: 942 us; the launch traced here: 937 us
  waiting for transfers between devices  476 us (51%)
  blocking collectives  307 us (33%)
  matrix products  63.5 us (7%)
  local copies, waits for them, and re-layouts  31.2 us (3%)
  other arithmetic  22.5 us (2%)
  starting transfers between devices  22.4 us (2%)
  between operations  14 us (1%)
    all_gather x4, blocking collectives, on_device(): key_piece = lax.all_gather(key_vecs, 'ctx', axis=0, tiled=True)  176 us
    all_gather x1, waiting for transfers between devices, on_device(): lax.all_gather(w_key[0], 'ctx', axis=0, tiled=True)  135 us
    all_gather x4, blocking collectives, on_device(): value_piece = lax.all_gather(values, 'ctx', axis=0, tiled=True)  131 us
    reduce_scatter x4, waiting for transfers between devices, on_device(): lax.psum_scatter(lax.dot_general(attended, output_weights, (((1,), (1,)),...  126 us
    all_gather x4, waiting for transfers between devices, on_device(): full_rows = lax.all_gather(current, 'tp', axis=1, tiled=True)  95.1 us
    all_gather x1, waiting for transfers between devices, on_device(): lax.all_gather(w_out[0], 'ctx', axis=0, tiled=True)  68.7 us
    all_gather x1, waiting for transfers between devices, on_device(): lax.all_gather(w_value[0], 'ctx', axis=0, tiled=True)  32.7 us
    dot_general x4, matrix products, on_device(): jnp.dot(normed, query_weights, preferred_element_type=jnp.float32)  24.7 us
  transfers between devices with their start and end apart: 15, of which 14 were waited for; matrix products, arithmetic and copies ran while one was open for 5% of the time, Pallas kernels for 0%

profile of v1, /device:TPU:1, one launch (start us, length us, event | category | flops | bytes accessed | tf_op | source)
XLA Modules:
  0.0 937.0 jit_solution(6654825240659565576)
XLA Ops:
  9.3 4.1 stack.18
  13.3 11.8 %all-to-all-start = ((bf16[16,256,1024]{1,2,0:T(8,128)(2,1)}), bf16[16,256,1024]{1,2,0:T(8,128)(2,1)}, u32[]{:S(2)}, u32[]{:S(2)}) async-start(bf16[16,256,1024]{1,2,0:T(8,128)(2,1)} %stack.18), calls=%async_computation | async-start | bytes 16777216 | tf_op jit(solution)/shard_map/all_to_all | solution.py:52
  27.3 18.0 %all-gather.18.cloned.1.call-done = bf16[1,128,4096]{2,1,0:T(8,128)(2,1)} async-done(((bf16[1,128,1024]{2,1,0:T(8,128)(2,1)}), bf16[1,128,4096]{2,1,0:T(8,128)(2,1)}) %all-gather.18.cloned.1.call-update) | async-done | bytes 1048592 | tf_op jit(solution)/shard_map/all_gather | solution.py:71
  46.9 134.5 %all-gather.20.cloned.1.call-done = bf16[1,4096,128]{2,1,0:T(8,128)(2,1)} async-done(((bf16[1,256,128]{2,1,0:T(8,128)(2,1)}), bf16[1,4096,128]{2,1,0:T(8,128)(2,1)}) %all-gather.20.cloned.1.call-update) | async-done | bytes 1048592 | tf_op jit(solution)/shard_map/all_gather | solution.py:54
  181.4 2.2 convolution_bitcast_fusion.3
  183.8 65.1 %all_gather.47 = bf16[2048,128]{0,1:T(8,128)(2,1)S(1)} all-gather(bf16[128,128]{0,1:T(8,128)(2,1)S(1)} %pad_maximum_fusion), channel_id=1, replica_groups=mesh['section'=4,'ctx'=16,'tp'=4] {'ctx'}, dimensions={0}, use_global_device_ids=true | all-gather | bytes 557056 | tf_op jit(solution)/shard_map/all_gather | solution.py:97
  248.9 32.7 %all-gather.22.cloned.1.call-done = bf16[1,4096,128]{2,1,0:T(8,128)(2,1)} async-done(((bf16[1,256,128]{2,1,0:T(8,128)(2,1)}), bf16[1,4096,128]{2,1,0:T(8,128)(2,1)}) %all-gather.22.cloned.1.call-update) | async-done | bytes 1048592 | tf_op jit(solution)/shard_map/all_gather | solution.py:55
  281.5 2.0 convolution_convert_fusion.3
  283.6 34.6 %all_gather.49 = bf16[2048,128]{1,0:T(8,128)(2,1)S(1)} all-gather(bf16[128,128]{1,0:T(8,128)(2,1)S(1)} %convolution_convert_fusion.3), channel_id=1, replica_groups=mesh['section'=4,'ctx'=16,'tp'=4] {'ctx'}, dimensions={0}, use_global_device_ids=true | all-gather | bytes 557056 | tf_op jit(solution)/shard_map/all_gather | solution.py:98
  318.2 12.3 %copy.58 = bf16[16,256,1024]{2,1,0:T(8,128)(2,1)} copy(bf16[16,256,1024]{1,2,0:T(8,128)(2,1)} %all-to-all-done) | data formatting | bytes 16777216 | tf_op jit(solution)/shard_map/all_to_all | solution.py:52
  330.5 11.7 %copy.59 = bf16[1024,4096]{1,0:T(8,128)(2,1)} copy(bf16[1024,4096]{0,1:T(8,128)(2,1)} %bitcast.290) | data formatting | bytes 16777216 | tf_op jit(solution)/shard_map/dot_general | solution.py:78
  342.3 6.2 fusion.78
  349.9 1.7 fusion.20
  351.7 1.7 fusion.105
  353.4 68.7 %all-gather.24.cloned.1.call-done = bf16[1,4096,1024]{2,1,0:T(8,128)(2,1)} async-done(((bf16[1,256,1024]{2,1,0:T(8,128)(2,1)}), bf16[1,4096,1024]{2,1,0:T(8,128)(2,1)}) %all-gather.24.cloned.1.call-update) | async-done | bytes 8388624 | tf_op jit(solution)/shard_map/all_gather | solution.py:56
  422.1 7.2 fusion.28
  429.5 21.0 %reduce-scatter.5.cloned.1.call-done = bf16[128,1024]{1,0:T(8,128)(2,1)} async-done(((bf16[128,4096]{1,0:T(8,128)(2,1)}), bf16[128,1024]{1,0:T(8,128)(2,1)}) %reduce-scatter.5.cloned.1.call-update) | async-done | bytes 262160 | tf_op jit(solution)/shard_map/reduce_scatter | solution.py:124
  451.5 3.1 collective-permute-start
  454.6 5.5 collective-permute-done
  461.5 25.4 %all-gather.12.cloned.1.call-done = bf16[128,4096]{1,0:T(8,128)(2,1)} async-done(((bf16[128,1024]{1,0:T(8,128)(2,1)}), bf16[128,4096]{1,0:T(8,128)(2,1)}) %all-gather.12.cloned.1.call-update) | async-done | bytes 1048592 | tf_op jit(solution)/shard_map/all_gather | solution.py:71
  488.5 6.2 fusion.72
  495.7 37.0 %all_gather.52 = bf16[2048,128]{0,1:T(8,128)(2,1)S(1)} all-gather(bf16[128,128]{0,1:T(8,128)(2,1)S(1)} %pad_maximum_fusion.1), channel_id=1, replica_groups=mesh['section'=4,'ctx'=16,'tp'=4] {'ctx'}, dimensions={0}, use_global_device_ids=true | all-gather | bytes 557056 | tf_op jit(solution)/shard_map/all_gather | solution.py:97
  533.3 32.2 %all_gather.53 = bf16[2048,128]{1,0:T(8,128)(2,1)S(1)} all-gather(bf16[128,128]{1,0:T(8,128)(2,1)S(1)} %convolution_convert_fusion.2), channel_id=1, replica_groups=mesh['section'=4,'ctx'=16,'tp'=4] {'ctx'}, dimensions={0}, use_global_device_ids=true | all-gather | bytes 557056 | tf_op jit(solution)/shard_map/all_gather | solution.py:98
  566.9 1.7 fusion.22
  568.6 1.7 fusion.99
  570.9 3.8 fusion.31
  574.8 34.9 %reduce-scatter.7.cloned.1.call-done = bf16[128,1024]{1,0:T(8,128)(2,1)} async-done(((bf16[128,4096]{1,0:T(8,128)(2,1)}), bf16[128,1024]{1,0:T(8,128)(2,1)}) %reduce-scatter.7.cloned.1.call-update) | async-done | bytes 262160 | tf_op jit(solution)/shard_map/reduce_scatter | solution.py:124
  610.8 3.1 collective-permute-start.1
  613.9 5.5 collective-permute-done.1
  620.4 25.9 %all-gather.14.cloned.1.call-done = bf16[128,4096]{1,0:T(8,128)(2,1)} async-done(((bf16[128,1024]{1,0:T(8,128)(2,1)}), bf16[128,4096]{1,0:T(8,128)(2,1)}) %all-gather.14.cloned.1.call-update) | async-done | bytes 1048592 | tf_op jit(solution)/shard_map/all_gather | solution.py:71
  647.9 6.2 fusion.70
  655.0 37.0 %all_gather.55 = bf16[2048,128]{0,1:T(8,128)(2,1)S(1)} all-gather(bf16[128,128]{0,1:T(8,128)(2,1)S(1)} %pad_maximum_fusion.2), channel_id=1, replica_groups=mesh['section'=4,'ctx'=16,'tp'=4] {'ctx'}, dimensions={0}, use_global_device_ids=true | all-gather | bytes 557056 | tf_op jit(solution)/shard_map/all_gather | solution.py:97
  692.6 32.1 %all_gather.56 = bf16[2048,128]{1,0:T(8,128)(2,1)S(1)} all-gather(bf16[128,128]{1,0:T(8,128)(2,1)S(1)} %convolution_convert_fusion.1), channel_id=1, replica_groups=mesh['section'=4,'ctx'=16,'tp'=4] {'ctx'}, dimensions={0}, use_global_device_ids=true | all-gather | bytes 557056 | tf_op jit(solution)/shard_map/all_gather | solution.py:98
  726.1 1.7 fusion.24
  727.8 1.7 fusion.93
  730.1 3.8 fusion.34
  734.0 34.9 %reduce-scatter.9.cloned.1.call-done = bf16[128,1024]{1,0:T(8,128)(2,1)} async-done(((bf16[128,4096]{1,0:T(8,128)(2,1)}), bf16[128,1024]{1,0:T(8,128)(2,1)}) %reduce-scatter.9.cloned.1.call-update) | async-done | bytes 262160 | tf_op jit(solution)/shard_map/reduce_scatter | solution.py:124
  769.9 3.1 collective-permute-start.2
  773.1 5.5 collective-permute-done.2
  779.6 25.8 %all-gather.16.cloned.1.call-done = bf16[128,4096]{1,0:T(8,128)(2,1)} async-done(((bf16[128,1024]{1,0:T(8,128)(2,1)}), bf16[128,4096]{1,0:T(8,128)(2,1)}) %all-gather.16.cloned.1.call-update) | async-done | bytes 1048592 | tf_op jit(solution)/shard_map/all_gather | solution.py:71
  805.4 1.6 fusion.62
  807.0 6.2 fusion.68
  814.1 37.0 %all_gather.58 = bf16[2048,128]{0,1:T(8,128)(2,1)S(1)} all-gather(bf16[128,128]{0,1:T(8,128)(2,1)S(1)} %pad_maximum_fusion.3), channel_id=1, replica_groups=mesh['section'=4,'ctx'=16,'tp'=4] {'ctx'}, dimensions={0}, use_global_device_ids=true | all-gather | bytes 557056 | tf_op jit(solution)/shard_map/all_gather | solution.py:97
  851.7 32.2 %all_gather.59 = bf16[2048,128]{1,0:T(8,128)(2,1)S(1)} all-gather(bf16[128,128]{1,0:T(8,128)(2,1)S(1)} %convolution_convert_fusion), channel_id=1, replica_groups=mesh['section'=4,'ctx'=16,'tp'=4] {'ctx'}, dimensions={0}, use_global_device_ids=true | all-gather | bytes 557056 | tf_op jit(solution)/shard_map/all_gather | solution.py:98
  885.4 1.7 fusion.26
  887.1 1.7 fusion.87
  889.4 3.8 fusion.37
  893.2 34.9 %reduce-scatter.11.cloned.1.call-done = bf16[128,1024]{1,0:T(8,128)(2,1)} async-done(((bf16[128,4096]{1,0:T(8,128)(2,1)}), bf16[128,1024]{1,0:T(8,128)(2,1)}) %reduce-scatter.11.cloned.1.call-update) | async-done | bytes 262160 | tf_op jit(solution)/shard_map/reduce_scatter | solution.py:124
  (119 shorter events, 30.2 us)
Async XLA Ops:
  6.5 38.8 %all-gather.18.cloned.1.call-start = ((), (), s32[]{:S(2)}) async-start(), calls=%async_computation.12 | async-start | bytes 1310720 | tf_op jit(solution)/shard_map/all_gather | solution.py:71
  7.3 174.1 %all-gather.20.cloned.1.call-start = ((), (), s32[]{:S(2)}) async-start(), calls=%async_computation.13 | async-start | bytes 1114112 | tf_op jit(solution)/shard_map/all_gather | solution.py:54
  13.3 13.2 %copy-start.10 = (s32[32]{0:T(128)S(1)}, s32[32]{0:T(128)}, u32[]{:S(2)}) copy-start(s32[32]{0:T(128)} %param.10) | copy-start | bytes 388
  13.3 168.1 %copy-start.9 = (f32[1,4096]{1,0:T(1,128)S(1)}, f32[1,4096]{1,0:T(1,128)}, u32[]{:S(2)}) copy-start(f32[1,4096]{1,0:T(1,128)} %param.11) | copy-start | bytes 49156
  13.3 304.9 %all-to-all-start = ((bf16[16,256,1024]{1,2,0:T(8,128)(2,1)}), bf16[16,256,1024]{1,2,0:T(8,128)(2,1)}, u32[]{:S(2)}, u32[]{:S(2)}) async-start(bf16[16,256,1024]{1,2,0:T(8,128)(2,1)} %stack.18), calls=%async_computation | async-start | bytes 16777216 | tf_op jit(solution)/shard_map/all_to_all | solution.py:52
  25.1 256.4 %all-gather.22.cloned.1.call-start = ((), (), s32[]{:S(2)}) async-start(), calls=%async_computation.14 | async-start | bytes 1114112 | tf_op jit(solution)/shard_map/all_gather | solution.py:55
  25.8 396.3 %all-gather.24.cloned.1.call-start = ((), (), s32[]{:S(2)}) async-start(), calls=%async_computation.15 | async-start | bytes 8912896 | tf_op jit(solution)/shard_map/all_gather | solution.py:56
  26.4 424.0 %reduce-scatter.5.cloned.1.call-start = ((), (), s32[]{:S(2)}) async-start(), calls=%async_computation.5 | async-start | bytes 1310720 | tf_op jit(solution)/shard_map/reduce_scatter | solution.py:124
  330.5 11.7 %copy-start = (bf16[1,128,4096]{2,1,0:T(8,128)(2,1)S(1)}, bf16[1,128,4096]{2,1,0:T(8,128)(2,1)}, u32[]{:S(2)}) copy-start(bf16[1,128,4096]{2,1,0:T(8,128)(2,1)} %all-gather.18.cloned.1.call-done) | copy-start | bytes 3145732
  353.4 97.1 %copy-start.7 = (bf16[1,128,1024]{2,1,0:T(8,128)(2,1)S(1)}, bf16[1,128,1024]{2,1,0:T(8,128)(2,1)}, u32[]{:S(2)}) copy-start(bf16[1,128,1024]{2,1,0:T(8,128)(2,1)} %param.8) | copy-start | bytes 786436
  353.4 106.8 %copy-start.8 = (bf16[3,128,1024]{2,1,0:T(8,128)(2,1)S(1)}, bf16[3,128,1024]{2,1,0:T(8,128)(2,1)}, u32[]{:S(2)}) copy-start(bf16[3,128,1024]{2,1,0:T(8,128)(2,1)} %param.9) | copy-start | bytes 2359300
  429.4 65.4 %copy-start.11 = (bf16[1,4096,128]{2,1,0:T(8,128)(2,1)S(1)}, bf16[1,4096,128]{2,1,0:T(8,128)(2,1)}, u32[]{:S(2)}) copy-start(bf16[1,4096,128]{2,1,0:T(8,128)(2,1)} %all-gather.20.cloned.1.call-done) | copy-start | bytes 3145732
  429.4 57.5 %all-gather.12.cloned.1.call-start = ((), (), s32[]{:S(2)}) async-start(), calls=%async_computation.6 | async-start | bytes 1310720 | tf_op jit(solution)/shard_map/all_gather | solution.py:71
  451.5 8.7 collective-permute-start
  460.9 148.8 %reduce-scatter.7.cloned.1.call-start = ((), (), s32[]{:S(2)}) async-start(), calls=%async_computation.7 | async-start | bytes 1310720 | tf_op jit(solution)/shard_map/reduce_scatter | solution.py:124
  486.9 7.9 copy-start.2
  488.5 44.2 %copy-start.12 = (bf16[1,4096,128]{2,1,0:T(8,128)(2,1)S(1)}, bf16[1,4096,128]{2,1,0:T(8,128)(2,1)}, u32[]{:S(2)}) copy-start(bf16[1,4096,128]{2,1,0:T(8,128)(2,1)} %all-gather.22.cloned.1.call-done) | copy-start | bytes 3145732
  566.9 3.4 slice-start
  568.6 2.3 slice-start.1
  570.3 39.4 %copy-start.5 = (bf16[128,1024]{1,0:T(8,128)(2,1)S(1)}, bf16[128,1024]{1,0:T(8,128)(2,1)}, u32[]{:S(2)}) copy-start(bf16[128,1024]{1,0:T(8,128)(2,1)} %bitcast_select_fusion.6) | copy-start | bytes 786436
  574.8 71.5 %all-gather.14.cloned.1.call-start = ((), (), s32[]{:S(2)}) async-start(), calls=%async_computation.8 | async-start | bytes 1310720 | tf_op jit(solution)/shard_map/all_gather | solution.py:71
  610.8 8.6 collective-permute-start.1
  620.2 148.8 %reduce-scatter.9.cloned.1.call-start = ((), (), s32[]{:S(2)}) async-start(), calls=%async_computation.9 | async-start | bytes 1310720 | tf_op jit(solution)/shard_map/reduce_scatter | solution.py:124
  646.3 7.9 copy-start.3
  647.9 44.2 %copy-start.13 = (bf16[1,4096,128]{2,1,0:T(8,128)(2,1)S(1)}, bf16[1,4096,128]{2,1,0:T(8,128)(2,1)}, u32[]{:S(2)}) copy-start(bf16[1,4096,128]{2,1,0:T(8,128)(2,1)} %all-gather.22.cloned.1.call-done) | copy-start | bytes 3145732
  726.1 3.4 slice-start.2
  727.8 2.3 slice-start.3
  729.6 39.4 %copy-start.6 = (bf16[128,1024]{1,0:T(8,128)(2,1)S(1)}, bf16[128,1024]{1,0:T(8,128)(2,1)}, u32[]{:S(2)}) copy-start(bf16[128,1024]{1,0:T(8,128)(2,1)} %bitcast_select_fusion.5) | copy-start | bytes 786436
  734.0 71.4 %all-gather.16.cloned.1.call-start = ((), (), s32[]{:S(2)}) async-start(), calls=%async_computation.10 | async-start | bytes 1310720 | tf_op jit(solution)/shard_map/all_gather | solution.py:71
  769.9 8.7 collective-permute-start.2
  779.3 148.8 %reduce-scatter.11.cloned.1.call-start = ((), (), s32[]{:S(2)}) async-start(), calls=%async_computation.11 | async-start | bytes 1310720 | tf_op jit(solution)/shard_map/reduce_scatter | solution.py:124
  805.4 7.9 copy-start.1
  807.0 44.2 %copy-start.14 = (bf16[1,4096,128]{2,1,0:T(8,128)(2,1)S(1)}, bf16[1,4096,128]{2,1,0:T(8,128)(2,1)}, u32[]{:S(2)}) copy-start(bf16[1,4096,128]{2,1,0:T(8,128)(2,1)} %all-gather.22.cloned.1.call-done) | copy-start | bytes 3145732
  885.4 3.5 slice-start.4
  887.1 2.3 slice-start.5
  888.8 39.3 %copy-start.4 = (bf16[128,1024]{1,0:T(8,128)(2,1)S(1)}, bf16[128,1024]{1,0:T(8,128)(2,1)}, u32[]{:S(2)}) copy-start(bf16[128,1024]{1,0:T(8,128)(2,1)} %bitcast_select_fusion.4) | copy-start | bytes 786436
Sparse Core Ops, SparseCore 0:
  9.1 36.1 all-gather.17
  47.9 133.4 all-gather.19
  184.0 97.4 all-gather.21
  284.0 138.1 all-gather.23
  429.5 20.8 reduce-scatter.4
  461.0 25.8 all-gather.11
  574.9 34.7 reduce-scatter.6
  620.3 25.9 all-gather.13
  734.1 34.7 reduce-scatter.8
  779.5 25.8 all-gather.15
  893.4 34.6 reduce-scatter.10
